TPU v7x, 128 devices: a whole 4x4x4 slice. The times are simulated.
128 devices in a mesh: tile: 64 (over z, y, x), slide: 2 (over core).
Axes of the slice: x: 4, y: 4, z: 4, core: 2. Of those that a mesh axis runs over, the one named last changes fastest.
Arguments:
- features: bfloat16 [256, 32, 32, 256], P(('slide', 'tile')), parts along dimension 0, may hold values from -8 to 8
- neighbours: int32 [256, 8], P(('slide', 'tile')), parts along dimension 0, may hold values from 0 to 128, as said below
- conv_weight: bfloat16 [3, 3, 256, 256], replicated, may hold values from -0.125 to 0.125
- patch_weight: bfloat16 [4096, 768], replicated, may hold values from -1 to 1
- query_weight: bfloat16 [768, 768], replicated, may hold values from -2 to 2
- key_weight: bfloat16 [768, 768], replicated, may hold values from -2 to 2
- value_weight: bfloat16 [768, 768], replicated, may hold values from -0.21875 to 0.21875
- output_weight: bfloat16 [768, 768], replicated, may hold values from -0.21875 to 0.21875
- cotangent: bfloat16 [16384, 768], P(('slide', 'tile')), parts along dimension 0, may hold values from -6 to 6
Outputs:
- mixed: bfloat16 [16384, 768], P(('slide', 'tile')), parts along dimension 0
- output_grad: float32 [1536, 768], P('slide'), parts along dimension 0
There are 2 independent parts, one for each index of `slide`. A program takes and returns all parts, laid end to end along the dimension named above; an argument that names none is the same for every part. Nothing has to cross between parts.
Inputs may be any that keep to these rules, and one draw needn't show every extreme that they name: Tiles are tissue cells of a grid 16 cells wide; the tile numbers are given to the tissue cells in a drawn order, so neighbours may have any numbers; each entry is the index of the tissue tile at that grid offset, or 128.
All inputs are finite; a program needn't handle non-finite values.
Results may differ from a plain program's by a relative error of at most 0.02.
Values may be sent and summed in bfloat16 or wider, within the bound.
No kernel may reach another device: no remote copies, remote signals or barrier semaphores. Data moves between devices by JAX's collectives and lax.ppermute only.
A program may use at most 192 MiB of HBM per device.

v0:
```python
import jax
import jax.numpy as jnp
from jax import lax
from jax.sharding import PartitionSpec as P

PATCH = 4
HEADS = 12
HD = 64


def tile_faces(maps):
    return jnp.stack([maps[:, 0], maps[:, -1], maps[:, :, 0], maps[:, :, -1]], axis=1)


def pad_tiles(maps, all_faces, links):
    upper = all_faces[links[:, 1], 1]
    lower = all_faces[links[:, 6], 0]
    left_col = all_faces[links[:, 3], 3]
    right_col = all_faces[links[:, 4], 2]
    corner_ul = all_faces[links[:, 0], 1, -1]
    corner_ur = all_faces[links[:, 2], 1, 0]
    corner_dl = all_faces[links[:, 5], 0, -1]
    corner_dr = all_faces[links[:, 7], 0, 0]
    top_row = jnp.concatenate([corner_ul[:, None], upper, corner_ur[:, None]], axis=1)
    bottom_row = jnp.concatenate([corner_dl[:, None], lower, corner_dr[:, None]], axis=1)
    middle = jnp.concatenate([left_col[:, :, None], maps, right_col[:, :, None]], axis=2)
    return jnp.concatenate([top_row[:, None], middle, bottom_row[:, None]], axis=1)


def conv_tiles(padded, kernel):
    count = padded.shape[0]
    side = padded.shape[1] - 2
    chans = padded.shape[3]
    total = jnp.zeros((count * side * side, kernel.shape[3]), jnp.float32)
    for row_off in range(3):
        for col_off in range(3):
            window = padded[:, row_off : row_off + side, col_off : col_off + side, :].reshape(
                -1, chans
            )
            total = total + jnp.dot(
                window, kernel[row_off, col_off], preferred_element_type=jnp.float32
            )
    return jax.nn.gelu(total).astype(jnp.bfloat16).reshape(count, side, side, -1)


def patchify(hidden, patch):
    count, side, _, chans = hidden.shape
    blocks = side // patch
    grid = hidden.reshape(count, blocks, patch, blocks, patch, chans).transpose(0, 1, 3, 2, 4, 5)
    return grid.reshape(count * blocks * blocks, patch * patch * chans)


def local(
    features,
    neighbours,
    conv_weight,
    patch_weight,
    query_weight,
    key_weight,
    value_weight,
    output_weight,
    cotangent,
):
    local_faces = tile_faces(features)
    gathered = lax.all_gather(local_faces, "tile", axis=0, tiled=True)
    all_faces = jnp.concatenate(
        [gathered, jnp.zeros((1,) + gathered.shape[1:], jnp.bfloat16)], axis=0
    )
    padded = pad_tiles(features, all_faces, neighbours)
    hidden = conv_tiles(padded, conv_weight)
    tokens = jnp.dot(
        patchify(hidden, PATCH), patch_weight, preferred_element_type=jnp.float32
    ).astype(jnp.bfloat16)
    rows = tokens.shape[0]
    query = (
        jnp.dot(tokens, query_weight, preferred_element_type=jnp.float32)
        .astype(jnp.bfloat16)
        .reshape(rows, HEADS, HD)
    )
    scale = HD ** (-0.5)
    keys = jnp.dot(tokens, key_weight, preferred_element_type=jnp.float32).astype(jnp.bfloat16)
    values = jnp.dot(tokens, value_weight, preferred_element_type=jnp.float32).astype(jnp.bfloat16)
    top = jnp.full((HEADS, rows), -1e30, jnp.float32)
    key_heads = lax.all_gather(keys, "tile", axis=0, tiled=True).reshape(-1, HEADS, HD)
    value_heads = lax.all_gather(values, "tile", axis=0, tiled=True).reshape(-1, HEADS, HD)
    scores = (
        jnp.einsum("qhd,khd->hqk", query, key_heads, preferred_element_type=jnp.float32) * scale
    )
    new_top = jnp.maximum(top, jnp.max(scores, axis=-1))
    weights = jnp.exp(scores - new_top[..., None])
    total = jnp.sum(weights, axis=-1)
    accum = jnp.einsum(
        "hqk,khd->hqd",
        weights.astype(jnp.bfloat16),
        value_heads,
        preferred_element_type=jnp.float32,
    )
    top, total, accum = (new_top, total, accum)
    attended = (
        (accum / total[..., None]).transpose(1, 0, 2).reshape(rows, HEADS * HD).astype(jnp.bfloat16)
    )
    mixed = (
        tokens.astype(jnp.float32)
        + jnp.dot(attended, output_weight, preferred_element_type=jnp.float32)
    ).astype(jnp.bfloat16)
    grad_term = jnp.dot(attended.T, cotangent, preferred_element_type=jnp.float32)
    output_grad = lax.psum(grad_term, "tile")
    return (mixed, output_grad)


def solution(mesh):
    in_specs = (
        P(("slide", "tile"), None, None, None),
        P(("slide", "tile"), None),
        P(),
        P(),
        P(),
        P(),
        P(),
        P(),
        P(("slide", "tile"), None),
    )
    out_specs = (P(("slide", "tile"), None), P("slide", None))
    return jax.shard_map(local, mesh=mesh, in_specs=in_specs, out_specs=out_specs, check_vma=False)
```

profile of v0, /device:TPU:0, one launch (start us, length us, event | category | flops | bytes accessed | tf_op | source)
XLA Modules:
  0.0 506.7 jit_solution(2070060483644725372)
XLA Ops:
  7.2 0.0 copy-start
  7.2 0.0 all-gather.4.cloned.1.call-start
  7.2 1.2 fusion.78
  8.5 0.8 fusion.77
  9.3 0.7 pad_maximum_fusion.3
  9.9 0.0 all-gather.4.cloned.1.call-update
  10.0 0.0 all-gather.6.cloned.1.call-start
  10.0 1.3 fusion.68
  11.3 0.0 copy-start.2
  11.3 81.0 %all-gather.4.cloned.1.call-done = bf16[128,4,32,256]{3,2,1,0:T(8,128)(2,1)} async-done(((bf16[2,4,32,256]{3,2,1,0:T(8,128)(2,1)}), bf16[128,4,32,256]{3,2,1,0:T(8,128)(2,1)}) %all-gather.4.cloned.1.call-update) | async-done | bytes 8388624 | tf_op jit(solution)/shard_map/all_gather | solution.py:65
  92.3 8.5 %concatenate.53 = bf16[129,4,32,256]{3,2,1,0:T(8,128)(2,1)} pad(bf16[128,4,32,256]{3,2,1,0:T(8,128)(2,1)} %all-gather.4.cloned.1.call-done, bf16[]{:T(256)} %constant.15.clone.1), padding=0_1x0_0x0_0x0_0 | pad | bytes 16842754 | tf_op jit(solution)/shard_map/concatenate | solution.py:66
  100.8 3.9 gather_fusion.1
  104.8 1.5 gather_fusion
  106.3 1.5 gather_fusion.2
  107.8 3.9 gather_fusion.6
  111.7 1.5 gather_fusion.5
  113.2 1.5 gather_fusion.7
  114.7 3.9 gather_fusion.3
  118.6 0.1 copy.43
  118.7 4.0 gather_fusion.4
  122.7 0.1 copy.44
  122.7 1.2 pad_maximum_fusion.1
  124.0 1.7 pad_maximum_fusion
  125.7 0.8 fusion.76
  126.5 0.0 copy-start.5
  126.5 0.8 fusion.75
  127.2 0.5 copy-done.5
  127.7 0.4 fusion.32
  128.2 0.4 convolution_add_fusion.7
  128.6 0.4 convolution_add_fusion.6
  129.1 0.4 convolution_add_fusion.5
  129.5 0.4 convolution_add_fusion.4
  129.9 0.4 convolution_add_fusion.3
  130.4 0.4 convolution_add_fusion.2
  130.8 0.5 convolution_add_fusion.1
  131.3 0.9 fusion.13
  132.2 0.3 reshape_reshape.3
  132.5 0.4 copy.60
  132.9 0.8 reshape.58
  133.7 3.8 convolution_convert_fusion.3
  137.5 0.0 copy-start.3
  137.5 1.0 convolution_convert_fusion.1
  138.5 0.0 all-gather.6.cloned.1.call-update
  138.6 0.0 all-gather.8.cloned.1.call-start
  138.6 2.3 convolution_convert_fusion
  140.9 0.0 all-gather.8.cloned.1.call-update
  140.9 0.2 all-reduce.8.cloned.1.call-start
  141.1 0.0 copy-done.3
  141.2 0.3 convolution_convert_fusion.2
  141.5 0.2 copy.52
  141.7 87.6 %all-gather.6.cloned.1.call-done = bf16[8192,768]{1,0:T(8,128)(2,1)} async-done(((bf16[128,768]{1,0:T(8,128)(2,1)}), bf16[8192,768]{1,0:T(8,128)(2,1)}) %all-gather.6.cloned.1.call-update) | async-done | bytes 12582928 | tf_op jit(solution)/shard_map/all_gather | solution.py:84
  229.2 15.8 %copy.53 = bf16[8192,768]{0,1:T(8,128)(2,1)} copy(bf16[8192,768]{1,0:T(8,128)(2,1)} %all-gather.6.cloned.1.call-done) | data formatting | bytes 25165824 | tf_op jit(solution)/shard_map/all_gather | solution.py:84
  245.0 22.0 %multiply_reduce_fusion = (f32[12,128]{1,0:T(8,128)S(1)}, f32[12,128,8192]{2,1,0:T(8,128)}) fusion(bf16[128,12,64]{0,2,1:T(8,128)(2,1)S(1)} %bitcast.106, bf16[8192,12,64]{0,2,1:T(8,128)(2,1)} %bitcast.92), kind=kOutput, calls=%fused_computation.9 | convolution fusion | flops 1635777024 | bytes 63117312 | tf_op jit(solution)/shard_map/qhd,khd->hqk/dot_general | solution.py:87
  267.0 21.7 %fusion = f32[12,128]{1,0:T(8,128)S(1)} fusion(f32[12,128,8192]{2,1,0:T(8,128)} %get-tuple-element.25, f32[12,128]{1,0:T(8,128)S(1)} %broadcast_maximum_fusion), kind=kLoop, calls=%fused_computation.10 | loop fusion | flops 37747200 | bytes 50343936 | tf_op jit(solution)/shard_map/reduce_sum | solution.py:91
  288.8 34.3 %all-gather.8.cloned.1.call-done = bf16[8192,768]{1,0:T(8,128)(2,1)} async-done(((bf16[128,768]{1,0:T(8,128)(2,1)}), bf16[8192,768]{1,0:T(8,128)(2,1)}) %all-gather.8.cloned.1.call-update) | async-done | bytes 12582928 | tf_op jit(solution)/shard_map/all_gather | solution.py:85
  323.1 15.8 %copy.54 = bf16[8192,768]{0,1:T(8,128)(2,1)} copy(bf16[8192,768]{1,0:T(8,128)(2,1)} %all-gather.8.cloned.1.call-done) | data formatting | bytes 25165824 | tf_op jit(solution)/shard_map/all_gather | solution.py:85
  338.9 22.2 %fusion.21 = bf16[128,12,64]{0,2,1:T(8,128)(2,1)S(1)} fusion(bf16[8192,12,64]{0,2,1:T(8,128)(2,1)} %bitcast.93, f32[12,128,8192]{2,1,0:T(8,128)} %get-tuple-element.25, f32[12,128]{1,0:T(8,128)S(1)} %broadcast_maximum_fusion, f32[128,12]{0,1:T(8,128)S(1)} %bitcast.109), kind=kOutput, calls=%fused_computation.42 | convolution fusion | flops 1648558080 | bytes 63123456 | tf_op jit(solution)/shard_map/hqk,khd->hqd/dot_general | solution.py:92
  361.1 0.0 copy-start.4
  361.1 1.9 fusion.79
  363.0 0.0 all-reduce.8.cloned.1.call-update
  363.0 0.0 copy-start.1
  363.0 1.0 fusion.17
  364.1 132.8 %all-reduce.8.cloned.1.call-done = f32[768,768]{1,0:T(8,128)} async-done(((f32[768,768]{1,0:T(8,128)}), f32[768,768]{1,0:T(8,128)}) %all-reduce.8.cloned.1.call-update) | async-done | bytes 2359312 | tf_op jit(solution)/shard_map/psum | solution.py:107
  496.9 3.2 copy.62
  (14 shorter events, 0.1 us)
Async XLA Ops:
  7.2 130.3 %copy-start = (bf16[768,768]{1,0:T(8,128)(2,1)S(1)}, bf16[768,768]{1,0:T(8,128)(2,1)}, u32[]{:S(2)}) copy-start(bf16[768,768]{1,0:T(8,128)(2,1)} %param.14) | copy-start | bytes 3538948
  7.2 85.1 %all-gather.4.cloned.1.call-start = ((), (), s32[]{:S(2)}) async-start(), calls=%async_computation | async-start | bytes 8519680 | tf_op jit(solution)/shard_map/all_gather | solution.py:65
  10.0 219.3 %all-gather.6.cloned.1.call-start = ((), (), s32[]{:S(2)}) async-start(), calls=%async_computation.1 | async-start | bytes 12779520 | tf_op jit(solution)/shard_map/all_gather | solution.py:84
  11.3 111.4 %copy-start.2 = (bf16[2,32,32,256]{3,2,1,0:T(8,128)(2,1)S(1)}, bf16[2,32,32,256]{3,2,1,0:T(8,128)(2,1)}, u32[]{:S(2)}) copy-start(bf16[2,32,32,256]{3,2,1,0:T(8,128)(2,1)} %param.9) | copy-start | bytes 3145732
  126.5 1.3 copy-start.5
  137.5 3.6 copy-start.3
  138.6 184.5 %all-gather.8.cloned.1.call-start = ((), (), s32[]{:S(2)}) async-start(), calls=%async_computation.2 | async-start | bytes 12779520 | tf_op jit(solution)/shard_map/all_gather | solution.py:85
  140.9 356.0 %all-reduce.8.cloned.1.call-start = ((), (), s32[]{:S(2)}) async-start(), calls=%async_computation.3 | async-start | bytes 4718592 | tf_op jit(solution)/shard_map/psum | solution.py:107
  338.9 22.2 %copy-start.6 = (bf16[128,768]{1,0:T(8,128)(2,1)S(1)}, bf16[128,768]{1,0:T(8,128)(2,1)}, u32[]{:S(2)}) copy-start(bf16[128,768]{1,0:T(8,128)(2,1)} %param.17) | copy-start | bytes 589828
  361.1 1.9 copy-start.4
  363.0 137.1 %copy-start.1 = (bf16[768,768]{1,0:T(8,128)(2,1)S(1)}, bf16[768,768]{1,0:T(8,128)(2,1)}, u32[]{:S(2)}) copy-start(bf16[768,768]{1,0:T(8,128)(2,1)} %param.14) | copy-start | bytes 3538948
Sparse Core Ops, SparseCore 0:
  11.4 80.8 all-gather.3
  138.7 90.4 all-gather.5
  232.5 90.5 all-gather.7
  363.1 133.7 all-reduce.7
where the time goes:
time: 508 us; the launch traced here: 507 us
  waiting for transfers between devices  336 us (66%)
  local copies, waits for them, and re-layouts  70.9 us (14%)
  matrix products  58.9 us (12%)
  other arithmetic  26.6 us (5%)
  between operations  14 us (3%)
    psum x1, waiting for transfers between devices, local(): output_grad = lax.psum(grad_term, 'tile')  133 us
    all_gather x1, waiting for transfers between devices, local(): lax.all_gather(keys, 'tile', axis=0, tiled=True).reshape(-1, HEADS, HD)  87.6 us
    all_gather x1, waiting for transfers between devices, local(): gathered = lax.all_gather(local_faces, 'tile', axis=0, tiled=True)  81 us
    all_gather x1, waiting for transfers between devices, local(): lax.all_gather(values, 'tile', axis=0, tiled=True).reshape(-1, HEADS, HD)  34.3 us
    dot_general x1, matrix products, local(): jnp.einsum('hqk,khd->hqd', weights.astype(jnp.bfloat16), value_heads, pre...  22.2 us
    dot_general x1, matrix products, local(): jnp.einsum('qhd,khd->hqk', query, key_heads, preferred_element_type=jnp.f...  22 us
    reduce_sum x1, other arithmetic, local(): total = jnp.sum(weights, axis=-1)  21.7 us
    all_gather x1, local copies, waits for them, and re-layouts, local(): lax.all_gather(keys, 'tile', axis=0, tiled=True).reshape(-1, HEADS, HD)  15.8 us
  transfers between devices with their start and end apart: 4, of which 4 were waited for; matrix products, arithmetic and copies ran while one was open for 13% of the time, Pallas kernels for 0%

commit v1 on v0

--- a/solution.py
+++ b/solution.py
@@ -81,7 +81,14 @@
     keys = jnp.dot(tokens, key_weight, preferred_element_type=jnp.float32).astype(jnp.bfloat16)
     values = jnp.dot(tokens, value_weight, preferred_element_type=jnp.float32).astype(jnp.bfloat16)
     top = jnp.full((HEADS, rows), -1e30, jnp.float32)
-    key_heads = lax.all_gather(keys, "tile", axis=0, tiled=True).reshape(-1, HEADS, HD)
+
+    def touch_runs(inputs, mesh_dim):
+        tmp = jnp.concatenate(
+            lax.all_to_all(jnp.stack([inputs] * lax.axis_size(mesh_dim), 0), mesh_dim, 0, 0), 0
+        )
+        return tmp
+
+    key_heads = touch_runs(keys, "tile").reshape(-1, HEADS, HD)
     value_heads = lax.all_gather(values, "tile", axis=0, tiled=True).reshape(-1, HEADS, HD)
     scores = (
         jnp.einsum("qhd,khd->hqk", query, key_heads, preferred_element_type=jnp.float32) * scale

time: 508 us -> 634 us (1.25)
  waiting for transfers between devices: 336 us -> 429 us
  local copies, waits for them, and re-layouts: 70.9 us -> 96.6 us
  starting transfers between devices: 0.35 us -> 9.09 us
    all_to_all x0 -> x1, waiting for transfers between devices: none -> 202 us  [touch_runs(): lax.all_to_all(jnp.stack([inputs] * lax.axis_size(mesh_dim), 0), mesh_dim...]
    all_gather x1 -> x0, waiting for transfers between devices: 87.6 us -> none  [local(): lax.all_gather(keys, 'tile', axis=0, tiled=True).reshape(-1, HEADS, HD)]
    all_gather x1, waiting for transfers between devices: 34.3 us -> 0.02 us  [local(): lax.all_gather(values, 'tile', axis=0, tiled=True).reshape(-1, HEADS, HD)]
    another operation x0 -> x2, local copies, waits for them, and re-layouts: none -> 26.8 us  [the longest x1 19.3 us: local(): key_heads = touch_runs(keys, 'tile').reshape(-1, HEADS, HD)]
    all_gather x1 -> x0, local copies, waits for them, and re-layouts: 15.8 us -> none  [local(): lax.all_gather(keys, 'tile', axis=0, tiled=True).reshape(-1, HEADS, HD)]
    all_to_all x0 -> x1, local copies, waits for them, and re-layouts: none -> 14.5 us  [touch_runs(): lax.all_to_all(jnp.stack([inputs] * lax.axis_size(mesh_dim), 0), mesh_dim...]
    psum x1, waiting for transfers between devices: 133 us -> 146 us  [local(): output_grad = lax.psum(grad_term, 'tile')]
    all_to_all x0 -> x1, starting transfers between devices: none -> 8.96 us  [touch_runs(): lax.all_to_all(jnp.stack([inputs] * lax.axis_size(mesh_dim), 0), mesh_dim...]
  transfers between devices with their start and end apart: 4 -> 4, of which waited for: 4 -> 3; matrix products, arithmetic and copies ran while one was open for 13% -> 14% of each run, Pallas kernels for 0% -> 0%
where the time goes in v1:
time: 634 us; the launch traced here: 633 us
  waiting for transfers between devices  429 us (68%)
  local copies, waits for them, and re-layouts  96.6 us (15%)
  matrix products  58 us (9%)
  other arithmetic  25.6 us (4%)
  between operations  14.1 us (2%)
  starting transfers between devices  9.09 us (1%)
    all_to_all x1, waiting for transfers between devices, touch_runs(): lax.all_to_all(jnp.stack([inputs] * lax.axis_size(mesh_dim), 0), mesh_dim...  202 us
    psum x1, waiting for transfers between devices, local(): output_grad = lax.psum(grad_term, 'tile')  146 us
    all_gather x1, waiting for transfers between devices, local(): gathered = lax.all_gather(local_faces, 'tile', axis=0, tiled=True)  81 us
    dot_general x1, matrix products, local(): jnp.einsum('hqk,khd->hqd', weights.astype(jnp.bfloat16), value_heads, pre...  22.2 us
    dot_general x1, matrix products, local(): jnp.einsum('qhd,khd->hqk', query, key_heads, preferred_element_type=jnp.f...  21.7 us
    reduce_sum x1, other arithmetic, local(): total = jnp.sum(weights, axis=-1)  20.5 us
    another operation x1, local copies, waits for them, and re-layouts, local(): key_heads = touch_runs(keys, 'tile').reshape(-1, HEADS, HD)  19.3 us
    all_gather x1, local copies, waits for them, and re-layouts, local(): lax.all_gather(values, 'tile', axis=0, tiled=True).reshape(-1, HEADS, HD)  15.8 us
  transfers between devices with their start and end apart: 4, of which 3 were waited for; matrix products, arithmetic and copies ran while one was open for 14% of the time, Pallas kernels for 0%

profile of v1, /device:TPU:0, one launch (start us, length us, event | category | flops | bytes accessed | tf_op | source)
XLA Modules:
  0.0 632.6 jit_solution(10034574884031518418)
XLA Ops:
  7.2 0.0 copy-start
  7.2 0.0 all-gather.3.cloned.1.call-start
  7.2 1.2 fusion.78
  8.5 0.8 fusion.77
  9.3 0.7 pad_maximum_fusion.3
  9.9 0.0 all-gather.3.cloned.1.call-update
  10.0 0.0 all-gather.5.cloned.1.call-start
  10.0 1.3 fusion.68
  11.3 0.0 copy-start.2
  11.3 81.0 %all-gather.3.cloned.1.call-done = bf16[128,4,32,256]{3,2,1,0:T(8,128)(2,1)} async-done(((bf16[2,4,32,256]{3,2,1,0:T(8,128)(2,1)}), bf16[128,4,32,256]{3,2,1,0:T(8,128)(2,1)}) %all-gather.3.cloned.1.call-update) | async-done | bytes 8388624 | tf_op jit(solution)/shard_map/all_gather | solution.py:65
  92.3 8.5 %concatenate.53 = bf16[129,4,32,256]{3,2,1,0:T(8,128)(2,1)} pad(bf16[128,4,32,256]{3,2,1,0:T(8,128)(2,1)} %all-gather.3.cloned.1.call-done, bf16[]{:T(256)} %constant.15.clone.1), padding=0_1x0_0x0_0x0_0 | pad | bytes 16842754 | tf_op jit(solution)/shard_map/concatenate | solution.py:66
  100.8 3.9 gather_fusion.1
  104.8 1.5 gather_fusion
  106.3 1.5 gather_fusion.2
  107.8 3.9 gather_fusion.6
  111.7 1.5 gather_fusion.5
  113.2 1.5 gather_fusion.7
  114.7 3.9 gather_fusion.3
  118.6 0.1 copy.43
  118.7 4.0 gather_fusion.4
  122.7 0.1 copy.44
  122.7 1.2 pad_maximum_fusion.1
  124.0 1.9 pad_maximum_fusion
  125.9 0.8 fusion.76
  126.6 0.0 copy-start.5
  126.7 0.8 fusion.75
  127.4 0.5 copy-done.5
  127.9 0.4 fusion.32
  128.3 0.4 convolution_add_fusion.7
  128.8 0.4 convolution_add_fusion.6
  129.2 0.4 convolution_add_fusion.5
  129.7 0.4 convolution_add_fusion.4
  130.1 0.4 convolution_add_fusion.3
  130.6 0.4 convolution_add_fusion.2
  131.0 0.4 convolution_add_fusion.1
  131.4 0.9 fusion.13
  132.4 0.3 reshape_reshape.6
  132.6 0.4 copy.61
  133.1 0.8 reshape.57
  133.9 3.8 convolution_convert_fusion.3
  137.7 1.0 convolution_convert_fusion
  138.7 0.0 all-gather.5.cloned.1.call-update
  138.7 1.6 convolution_convert_fusion.1
  140.3 0.2 copy.53
  140.5 7.5 %stack.5 = bf16[64,128,768]{1,2,0:T(8,128)(2,1)} broadcast(bf16[128,768]{0,1:T(8,128)(2,1)S(1)} %copy.53), dimensions={1,2} | broadcast | bytes 12779520 | tf_op jit(solution)/shard_map/stack | solution.py:87
  148.0 9.0 %all-to-all-start = ((bf16[64,128,768]{1,2,0:T(8,128)(2,1)}), bf16[64,128,768]{1,2,0:T(8,128)(2,1)}, u32[]{:S(2)}, u32[]{:S(2)}) async-start(bf16[64,128,768]{1,2,0:T(8,128)(2,1)} %stack.5), calls=%async_computation | async-start | bytes 25165824 | tf_op jit(solution)/shard_map/all_to_all | solution.py:87
  157.0 0.0 all-reduce.8.cloned.1.call-start
  157.0 0.3 convolution_convert_fusion.2
  157.4 0.2 copy.52
  157.5 202.2 %all-to-all-done = bf16[64,128,768]{1,2,0:T(8,128)(2,1)} async-done(((bf16[64,128,768]{1,2,0:T(8,128)(2,1)}), bf16[64,128,768]{1,2,0:T(8,128)(2,1)}, u32[]{:S(2)}, u32[]{:S(2)}) %all-to-all-start) | async-done | bytes 12582944 | tf_op jit(solution)/shard_map/all_to_all | solution.py:87
  359.8 14.5 %copy.54 = bf16[64,128,768]{1,0,2:T(8,128)(2,1)} copy(bf16[64,128,768]{1,2,0:T(8,128)(2,1)} %all-to-all-done) | data formatting | bytes 25165824 | tf_op jit(solution)/shard_map/all_to_all | solution.py:87
  374.3 19.3 %reshape_reshape.7 = bf16[8192,12,64]{0,2,1:T(8,128)(2,1)} reshape(bf16[64,128,768]{1,0,2:T(8,128)(2,1)} %copy.54) | data formatting | bytes 25165824 | tf_op jit(solution)/shard_map/reshape;reshape | solution.py:91
  393.6 21.7 %multiply_reduce_fusion = (f32[12,128]{1,0:T(8,128)S(1)}, f32[12,128,8192]{2,1,0:T(8,128)}) fusion(bf16[128,12,64]{0,2,1:T(8,128)(2,1)S(1)} %bitcast.106, bf16[8192,12,64]{0,2,1:T(8,128)(2,1)} %reshape_reshape.7), kind=kOutput, calls=%fused_computation.9 | convolution fusion | flops 1635777024 | bytes 63117312 | tf_op jit(solution)/shard_map/qhd,khd->hqk/dot_general | solution.py:94
  415.3 20.5 %fusion = f32[12,128]{1,0:T(8,128)S(1)} fusion(f32[12,128,8192]{2,1,0:T(8,128)} %get-tuple-element.25, f32[12,128]{1,0:T(8,128)S(1)} %broadcast_maximum_fusion), kind=kLoop, calls=%fused_computation.10 | loop fusion | flops 37747200 | bytes 50343936 | tf_op jit(solution)/shard_map/reduce_sum | solution.py:98
  435.8 0.0 all-gather.5.cloned.1.call-done
  435.8 15.8 %copy.55 = bf16[8192,768]{0,1:T(8,128)(2,1)} copy(bf16[8192,768]{1,0:T(8,128)(2,1)} %all-gather.5.cloned.1.call-done) | data formatting | bytes 25165824 | tf_op jit(solution)/shard_map/all_gather | solution.py:92
  451.6 22.2 %fusion.21 = bf16[128,12,64]{0,2,1:T(8,128)(2,1)S(1)} fusion(bf16[8192,12,64]{0,2,1:T(8,128)(2,1)} %bitcast.93, f32[12,128,8192]{2,1,0:T(8,128)} %get-tuple-element.25, f32[12,128]{1,0:T(8,128)S(1)} %broadcast_maximum_fusion, f32[128,12]{0,1:T(8,128)S(1)} %bitcast.109), kind=kOutput, calls=%fused_computation.42 | convolution fusion | flops 1648558080 | bytes 63123456 | tf_op jit(solution)/shard_map/hqk,khd->hqd/dot_general | solution.py:99
  473.9 0.0 copy-start.4
  473.9 1.9 fusion.79
  475.7 0.0 all-reduce.8.cloned.1.call-update
  475.8 0.0 copy-start.1
  475.8 1.0 fusion.17
  476.8 146.1 %all-reduce.8.cloned.1.call-done = f32[768,768]{1,0:T(8,128)} async-done(((f32[768,768]{1,0:T(8,128)}), f32[768,768]{1,0:T(8,128)}) %all-reduce.8.cloned.1.call-update) | async-done | bytes 2359312 | tf_op jit(solution)/shard_map/psum | solution.py:114
  622.9 3.2 copy.63
  (16 shorter events, 0.1 us)
Async XLA Ops:
  7.2 130.5 %copy-start = (bf16[768,768]{1,0:T(8,128)(2,1)S(1)}, bf16[768,768]{1,0:T(8,128)(2,1)}, u32[]{:S(2)}) copy-start(bf16[768,768]{1,0:T(8,128)(2,1)} %param.15) | copy-start | bytes 3538948
  7.2 85.1 %all-gather.3.cloned.1.call-start = ((), (), s32[]{:S(2)}) async-start(), calls=%async_computation.1 | async-start | bytes 8519680 | tf_op jit(solution)/shard_map/all_gather | solution.py:65
  10.0 425.9 %all-gather.5.cloned.1.call-start = ((), (), s32[]{:S(2)}) async-start(), calls=%async_computation.2 | async-start | bytes 12779520 | tf_op jit(solution)/shard_map/all_gather | solution.py:92
  11.3 111.4 %copy-start.2 = (bf16[2,32,32,256]{3,2,1,0:T(8,128)(2,1)S(1)}, bf16[2,32,32,256]{3,2,1,0:T(8,128)(2,1)}, u32[]{:S(2)}) copy-start(bf16[2,32,32,256]{3,2,1,0:T(8,128)(2,1)} %param.9) | copy-start | bytes 3145732
  126.6 1.3 copy-start.5
  148.0 9.0 %copy-start.3 = (bf16[768,768]{1,0:T(8,128)(2,1)S(1)}, bf16[768,768]{1,0:T(8,128)(2,1)}, u32[]{:S(2)}) copy-start(bf16[768,768]{1,0:T(8,128)(2,1)} %param.13) | copy-start | bytes 3538948
  148.0 211.8 %all-to-all-start = ((bf16[64,128,768]{1,2,0:T(8,128)(2,1)}), bf16[64,128,768]{1,2,0:T(8,128)(2,1)}, u32[]{:S(2)}, u32[]{:S(2)}) async-start(bf16[64,128,768]{1,2,0:T(8,128)(2,1)} %stack.5), calls=%async_computation | async-start | bytes 25165824 | tf_op jit(solution)/shard_map/all_to_all | solution.py:87
  157.0 465.9 %all-reduce.8.cloned.1.call-start = ((), (), s32[]{:S(2)}) async-start(), calls=%async_computation.3 | async-start | bytes 4718592 | tf_op jit(solution)/shard_map/psum | solution.py:114
  451.6 22.2 %copy-start.6 = (bf16[128,768]{1,0:T(8,128)(2,1)S(1)}, bf16[128,768]{1,0:T(8,128)(2,1)}, u32[]{:S(2)}) copy-start(bf16[128,768]{1,0:T(8,128)(2,1)} %param.17) | copy-start | bytes 589828
  473.9 1.9 copy-start.4
  475.8 150.3 %copy-start.1 = (bf16[768,768]{1,0:T(8,128)(2,1)S(1)}, bf16[768,768]{1,0:T(8,128)(2,1)}, u32[]{:S(2)}) copy-start(bf16[768,768]{1,0:T(8,128)(2,1)} %param.15) | copy-start | bytes 3538948
Sparse Core Ops, SparseCore 0:
  11.4 80.8 all-gather.2
  138.8 234.0 all-gather.4
  475.9 146.9 all-reduce.7
